TPU v7x, 256 devices: a whole 4x4x8 slice. The times are simulated.
256 devices in a mesh: row: 8 (over z_hi, core), col: 32 (over z_lo, x, y).
Axes of the slice: x: 4, y: 4, z: 8 (z_hi: 4, z_lo: 2; z = z_hi * 2 + z_lo), core: 2. Of those that a mesh axis runs over, the one named last changes fastest.
Arguments:
- panel_adj: float32 [14336, 512], P('row', 'col'), may hold values from -6 to 6
- inv_diag: float32 [512, 512], P('col'), may hold values from -0.25 to 0.25
- row_panel: float32 [512, 14336], P('row', 'col'), may hold values from -0.25 to 0.25
- trailing_adj: float32 [14336, 14336], P('row', 'col'), may hold values from -6 to 6
- trailing_factor: float32 [14336, 14336], P('row', 'col'), may hold values from -0.046875 to 0.046875
Outputs:
- trailing_new: float32 [14336, 14336], P('row', 'col')
- row_adj: float32 [512, 14336], P('row', 'col')
All inputs are finite; a program needn't handle non-finite values.
Results may differ from a plain program's by a relative error of at most 0.00007.
Values sent between devices are 32-bit elements; how exact they have to be, the bound alone decides.
A program may use at most 64 MiB of HBM per device.

v0:
```python
import jax
import jax.numpy as jnp
from jax import lax
from jax.sharding import PartitionSpec as P


def local(panel_adj, inv_diag, row_panel, trailing_adj, trailing_factor):
    highest = lax.Precision.HIGHEST
    inverse_all = lax.all_gather(inv_diag, "col", axis=0, tiled=True)
    scaled = jnp.dot(
        lax.all_gather(panel_adj, "col", axis=1, tiled=True),
        inverse_all,
        precision=highest,
        preferred_element_type=jnp.float32,
    )
    trailing_new = trailing_adj - jnp.dot(
        scaled,
        lax.all_gather(row_panel, "row", axis=0, tiled=True),
        precision=highest,
        preferred_element_type=jnp.float32,
    )
    terms_local = lax.dot_general(
        scaled,
        trailing_factor,
        (((0,), (0,)), ((), ())),
        precision=highest,
        preferred_element_type=jnp.float32,
    )
    row_adj = lax.psum_scatter(terms_local, "row", scatter_dimension=0, tiled=True)
    return (trailing_new, row_adj)


def solution(mesh):
    placed = (P("row", "col"), P("col", None), P("row", "col"), P("row", "col"), P("row", "col"))
    return jax.shard_map(
        local,
        mesh=mesh,
        in_specs=placed,
        out_specs=(P("row", "col"), P("row", "col")),
        check_vma=False,
    )
```

profile of v0, /device:TPU:8, one launch (start us, length us, event | category | flops | bytes accessed | tf_op | source)
XLA Modules:
  0.0 397.3 jit_solution(17460314961301271969)
XLA Ops:
  7.2 0.0 copy-start
  7.2 0.0 all-gather.5.cloned.1.call-start
  7.2 0.7 all-gather.5.cloned.1.call-update
  7.9 0.0 all-gather.3.cloned.1.call-start
  8.0 0.7 all-gather.3.cloned.1.call-update
  8.7 0.0 reduce-scatter.2.cloned.1.call-start
  8.7 157.2 %all-gather.5.cloned.1.call-done = f32[512,512]{1,0:T(8,128)} async-done(((f32[16,512]{1,0:T(8,128)}), f32[512,512]{1,0:T(8,128)}) %all-gather.5.cloned.1.call-update) | async-done | bytes 1048592 | tf_op jit(solution)/shard_map/all_gather | solution.py:9
  165.9 160.2 %all-gather.3.cloned.1.call-done = f32[1792,512]{0,1:T(8,128)} async-done(((f32[1792,16]{0,1:T(8,128)}), f32[1792,512]{0,1:T(8,128)}) %all-gather.3.cloned.1.call-update) | async-done | bytes 3670032 | tf_op jit(solution)/shard_map/all_gather | solution.py:11
  326.1 8.5 %fusion = f32[1792,512]{1,0:T(8,128)S(1)} fusion(f32[1792,512]{0,1:T(8,128)} %all-gather.3.cloned.1.call-done, f32[512,512]{1,0:T(8,128)} %all-gather.5.cloned.1.call-done), kind=kOutput, calls=%fused_computation.1 | convolution fusion | flops 5637144576 | bytes 8388608 | tf_op jit(solution)/shard_map/dot_general | solution.py:10
  334.6 0.0 copy-start.1
  334.7 1.8 copy-done.1
  336.4 0.0 copy-done
  336.4 0.0 copy-start.2
  336.4 13.0 %fusion.1 = f32[512,448]{1,0:T(8,128)} fusion(f32[1792,512]{1,0:T(8,128)S(1)} %fusion, f32[1792,448]{0,1:T(8,128)S(1)} %copy-done), kind=kOutput, calls=%fused_computation.2 | convolution fusion | flops 4932501504 | bytes 7798784 | tf_op jit(solution)/shard_map/dot_general | solution.py:22
  349.4 0.0 reduce-scatter.2.cloned.1.call-update
  349.5 0.0 copy-done.2
  349.5 20.0 %all_gather.11 = f32[512,448]{1,0:T(8,128)S(1)} all-gather(f32[64,448]{1,0:T(8,128)S(1)} %copy-done.2), channel_id=1, replica_groups=mesh['row'=8,'col'=32] {'row'}, dimensions={0}, use_global_device_ids=true | all-gather | bytes 1032192 | tf_op jit(solution)/shard_map/all_gather | solution.py:18
  369.4 10.4 %convolution_subtract_fusion = f32[1792,448]{0,1:T(8,128)} fusion(f32[1792,448]{0,1:T(8,128)} %param.8, f32[1792,512]{1,0:T(8,128)} %copy-done.1, f32[512,448]{1,0:T(8,128)S(1)} %all_gather.11), kind=kOutput, calls=%fused_computation | convolution fusion | flops 4933304320 | bytes 11010048 | tf_op jit(solution)/shard_map/dot_general | solution.py:16
  379.8 11.0 %reduce-scatter.2.cloned.1.call-done = f32[64,448]{1,0:T(8,128)} async-done(((f32[512,448]{1,0:T(8,128)}), f32[64,448]{1,0:T(8,128)}) %reduce-scatter.2.cloned.1.call-update) | async-done | bytes 114704 | tf_op jit(solution)/shard_map/reduce_scatter | solution.py:29
Async XLA Ops:
  7.2 329.3 %copy-start = (f32[1792,448]{0,1:T(8,128)S(1)}, f32[1792,448]{0,1:T(8,128)}, u32[]{:S(2)}) copy-start(f32[1792,448]{0,1:T(8,128)} %param.9) | copy-start | bytes 9633796
  7.2 158.7 %all-gather.5.cloned.1.call-start = ((), (), s32[]{:S(2)}) async-start(), calls=%async_computation.2 | async-start | bytes 1081344 | tf_op jit(solution)/shard_map/all_gather | solution.py:9
  7.9 318.2 %all-gather.3.cloned.1.call-start = ((), (), s32[]{:S(2)}) async-start(), calls=%async_computation.1 | async-start | bytes 3784704 | tf_op jit(solution)/shard_map/all_gather | solution.py:11
  8.7 382.1 %reduce-scatter.2.cloned.1.call-start = ((), (), s32[]{:S(2)}) async-start(), calls=%async_computation.3 | async-start | bytes 1179648 | tf_op jit(solution)/shard_map/reduce_scatter | solution.py:29
  334.6 1.8 copy-start.1
  336.4 13.0 %copy-start.2 = (f32[64,448]{1,0:T(8,128)S(1)}, f32[64,448]{1,0:T(8,128)}, u32[]{:S(2)}) copy-start(f32[64,448]{1,0:T(8,128)} %param.7) | copy-start | bytes 344068
Sparse Core Ops, SparseCore 0:
  9.8 156.0 all-gather.4
  167.6 158.3 all-gather.2
  349.6 41.1 reduce-scatter.1
where the time goes:
time: 397 us
  waiting for transfers between devices  330 us (83%)
  matrix products  31.9 us (8%)
  blocking collectives  20 us (5%)
  between operations  13.8 us (3%)
    all_gather x1, waiting for transfers between devices, local(): lax.all_gather(panel_adj, 'col', axis=1, tiled=True)  160 us
    all_gather x1, waiting for transfers between devices, local(): inverse_all = lax.all_gather(inv_diag, 'col', axis=0, tiled=True)  157 us
    all_gather x1, blocking collectives, local(): lax.all_gather(row_panel, 'row', axis=0, tiled=True)  20 us
    dot_general x1, matrix products, local(): lax.dot_general(scaled, trailing_factor, (((0,), (0,)), ((), ())), precis...  13 us
    reduce_scatter x1, waiting for transfers between devices, local(): lax.psum_scatter(terms_local, 'row', scatter_dimension=0, tiled=True)  11 us
    dot_general x1, matrix products, local(): jnp.dot(scaled, lax.all_gather(row_panel, 'row', axis=0, tiled=True), pre...  10.4 us
    dot_general x1, matrix products, local(): jnp.dot(lax.all_gather(panel_adj, 'col', axis=1, tiled=True), inverse_all...  8.55 us
  transfers between devices with their start and end apart: 3, of which 3 were waited for; matrix products, arithmetic and copies ran while one was open for 3% of the time, Pallas kernels for 0%

commit v1 on v0

--- a/solution.py
+++ b/solution.py
@@ -3,10 +3,15 @@
 from jax import lax
 from jax.sharding import PartitionSpec as P
 
+attach_results = lambda local_block, axis_key: jnp.concatenate(
+    lax.all_to_all(jnp.stack([local_block for _ in range(lax.psum(1, axis_key))]), axis_key, 0, 0),
+    0,
+)
+
 
 def local(panel_adj, inv_diag, row_panel, trailing_adj, trailing_factor):
     highest = lax.Precision.HIGHEST
-    inverse_all = lax.all_gather(inv_diag, "col", axis=0, tiled=True)
+    inverse_all = attach_results(inv_diag, "col")
     scaled = jnp.dot(
         lax.all_gather(panel_adj, "col", axis=1, tiled=True),
         inverse_all,

time: 397 us -> 245 us (0.62)
  waiting for transfers between devices: 330 us -> 149 us
  blocking collectives: 20 us -> 45.1 us
    all_gather x1 -> x0, waiting for transfers between devices: 157 us -> none  [local(): inverse_all = lax.all_gather(inv_diag, 'col', axis=0, tiled=True)]
    all_to_all x0 -> x1, blocking collectives: none -> 24.8 us  [lax.all_to_all(jnp.stack([local_block for _ in range(lax.psum(1, axis_key...]
    all_gather x1, waiting for transfers between devices: 160 us -> 138 us  [local(): lax.all_gather(panel_adj, 'col', axis=1, tiled=True)]
  transfers between devices with their start and end apart: 3 -> 2, of which waited for: 3 -> 2; matrix products, arithmetic and copies ran while one was open for 3% -> 5% of each run, Pallas kernels for 0% -> 0%
where the time goes in v1:
time: 245 us; the launch traced here: 243 us
  waiting for transfers between devices  149 us (61%)
  blocking collectives  45.1 us (18%)
  matrix products  31.9 us (13%)
  between operations  14.1 us (6%)
  local copies, waits for them, and re-layouts  2.84 us (1%)
    all_gather x1, waiting for transfers between devices, local(): lax.all_gather(panel_adj, 'col', axis=1, tiled=True)  138 us
    all_to_all x1, blocking collectives, lax.all_to_all(jnp.stack([local_block for _ in range(lax.psum(1, axis_key...  24.8 us
    all_gather x1, blocking collectives, local(): lax.all_gather(row_panel, 'row', axis=0, tiled=True)  20.2 us
    dot_general x1, matrix products, local(): lax.dot_general(scaled, trailing_factor, (((0,), (0,)), ((), ())), precis...  13 us
    reduce_scatter x1, waiting for transfers between devices, local(): lax.psum_scatter(terms_local, 'row', scatter_dimension=0, tiled=True)  10.7 us
    dot_general x1, matrix products, local(): jnp.dot(scaled, lax.all_gather(row_panel, 'row', axis=0, tiled=True), pre...  10.4 us
    dot_general x1, matrix products, local(): jnp.dot(lax.all_gather(panel_adj, 'col', axis=1, tiled=True), inverse_all...  8.54 us
  transfers between devices with their start and end apart: 2, of which 2 were waited for; matrix products, arithmetic and copies ran while one was open for 5% of the time, Pallas kernels for 0%

profile of v1, /device:TPU:8, one launch (start us, length us, event | category | flops | bytes accessed | tf_op | source)
XLA Modules:
  0.0 243.2 jit_solution(8438750449241671709)
XLA Ops:
  7.2 0.0 copy-start
  7.2 0.0 all-gather.2.cloned.1.call-start
  7.2 0.7 all-gather.2.cloned.1.call-update
  7.9 0.0 reduce-scatter.2.cloned.1.call-start
  8.0 1.0 stack.2
  9.0 24.8 %all_to_all.5 = f32[32,16,512]{2,1,0:T(8,128)} all-to-all(f32[32,16,512]{2,1,0:T(8,128)S(1)} %stack.2), channel_id=1, replica_groups=mesh['row'=8,'col'=32] {'col'}, dimensions={0} | all-to-all | bytes 2097152 | tf_op jit(solution)/shard_map/all_to_all | solution.py:7
  33.8 137.9 %all-gather.2.cloned.1.call-done = f32[1792,512]{0,1:T(8,128)} async-done(((f32[1792,16]{0,1:T(8,128)}), f32[1792,512]{0,1:T(8,128)}) %all-gather.2.cloned.1.call-update) | async-done | bytes 3670032 | tf_op jit(solution)/shard_map/all_gather | solution.py:16
  171.7 8.5 %fusion = f32[1792,512]{1,0:T(8,128)S(1)} fusion(f32[1792,512]{0,1:T(8,128)} %all-gather.2.cloned.1.call-done, f32[512,512]{1,0:T(8,128)} %bitcast.7), kind=kOutput, calls=%fused_computation.1 | convolution fusion | flops 5637144576 | bytes 8388608 | tf_op jit(solution)/shard_map/dot_general | solution.py:15
  180.3 0.0 copy-start.1
  180.3 1.8 copy-done.1
  182.1 0.0 copy-done
  182.1 0.0 copy-start.2
  182.1 13.0 %fusion.1 = f32[512,448]{1,0:T(8,128)} fusion(f32[1792,512]{1,0:T(8,128)S(1)} %fusion, f32[1792,448]{0,1:T(8,128)S(1)} %copy-done), kind=kOutput, calls=%fused_computation.2 | convolution fusion | flops 4932501504 | bytes 7798784 | tf_op jit(solution)/shard_map/dot_general | solution.py:27
  195.0 0.0 reduce-scatter.2.cloned.1.call-update
  195.1 0.0 copy-done.2
  195.1 20.2 %all_gather.7 = f32[512,448]{1,0:T(8,128)S(1)} all-gather(f32[64,448]{1,0:T(8,128)S(1)} %copy-done.2), channel_id=1, replica_groups=mesh['row'=8,'col'=32] {'row'}, dimensions={0}, use_global_device_ids=true | all-gather | bytes 1032192 | tf_op jit(solution)/shard_map/all_gather | solution.py:23
  215.3 10.4 %convolution_subtract_fusion = f32[1792,448]{0,1:T(8,128)} fusion(f32[1792,448]{0,1:T(8,128)} %param.8, f32[1792,512]{1,0:T(8,128)} %copy-done.1, f32[512,448]{1,0:T(8,128)S(1)} %all_gather.7), kind=kOutput, calls=%fused_computation | convolution fusion | flops 4933304320 | bytes 11010048 | tf_op jit(solution)/shard_map/dot_general | solution.py:21
  225.7 10.7 %reduce-scatter.2.cloned.1.call-done = f32[64,448]{1,0:T(8,128)} async-done(((f32[512,448]{1,0:T(8,128)}), f32[64,448]{1,0:T(8,128)}) %reduce-scatter.2.cloned.1.call-update) | async-done | bytes 114704 | tf_op jit(solution)/shard_map/reduce_scatter | solution.py:34
Async XLA Ops:
  7.2 174.9 %copy-start = (f32[1792,448]{0,1:T(8,128)S(1)}, f32[1792,448]{0,1:T(8,128)}, u32[]{:S(2)}) copy-start(f32[1792,448]{0,1:T(8,128)} %param.9) | copy-start | bytes 9633796
  7.2 164.6 %all-gather.2.cloned.1.call-start = ((), (), s32[]{:S(2)}) async-start(), calls=%async_computation.2 | async-start | bytes 3784704 | tf_op jit(solution)/shard_map/all_gather | solution.py:16
  7.9 228.5 %reduce-scatter.2.cloned.1.call-start = ((), (), s32[]{:S(2)}) async-start(), calls=%async_computation.3 | async-start | bytes 1179648 | tf_op jit(solution)/shard_map/reduce_scatter | solution.py:34
  180.3 1.8 copy-start.1
  182.1 13.0 %copy-start.2 = (f32[64,448]{1,0:T(8,128)S(1)}, f32[64,448]{1,0:T(8,128)}, u32[]{:S(2)}) copy-start(f32[64,448]{1,0:T(8,128)} %param.7) | copy-start | bytes 344068
Sparse Core Ops, SparseCore 0:
  9.8 161.9 all-gather.1
  195.2 41.1 reduce-scatter.1
